TPU v7x, 768 devices: a whole 4x8x12 slice. The times are simulated.
768 devices in a mesh: section: 48 (over x_lo, z, core), rows: 16 (over y, x_hi).
Axes of the slice: x: 4 (x_hi: 2, x_lo: 2; x = x_hi * 2 + x_lo), y: 8, z: 12, core: 2. Of those that a mesh axis runs over, the one named last changes fastest.
Arguments:
- activations: bfloat16 [48, 64, 32, 768], P('section', 'rows'), may hold values from -6 to 6
- cotangent: bfloat16 [48, 64, 32, 3072], P('section', None, None, 'rows'), may hold values from -6 to 6
- proj_weight: bfloat16 [768, 3072], P('section', 'rows'), may hold values from -0.21875 to 0.21875
- kernel_taps: bfloat16 [49, 768], replicated, may hold values from -0.875 to 0.875
- ln_gain: float32 [768], replicated, may hold values from 0.1 to 1.9
- ln_shift: float32 [768], replicated, may hold values from -3 to 3
- heights: int32 [48], P('section'), may hold values from 32 to 64, as said below
- widths: int32 [48], P('section'), may hold values from 16 to 32, as said below
Outputs:
- input_grad: bfloat16 [48, 64, 32, 768], P('section', 'rows')
- weight_grad: float32 [768, 3072], P('section', 'rows')
Inputs may be any that keep to these rules, and one draw needn't show every extreme that they name: `heights`: every image has at least half of 64 valid rows, and some image has all 64. `widths`: every image has at least half of 32 valid columns, and some image has all 32.
All inputs are finite; a program needn't handle non-finite values.
Results may differ from a plain program's by a relative error of at most 0.0049.
Values may be sent and summed in bfloat16 or wider, within the bound.
A program may use at most 32 MiB of HBM per device.

v0:
```python
import jax
import jax.numpy as jnp
from jax import lax
from jax.sharding import PartitionSpec as P

epsilon = 1e-06


def padded_2(block, sides, width):
    for axis, dim in sides:
        count = lax.axis_size(axis)
        forward = [(i, i + 1) for i in range(count - 1)]
        backward = [(target, source) for source, target in forward]
        low = lax.ppermute(
            lax.slice_in_dim(block, block.shape[dim] - width, None, axis=dim), axis, forward
        )
        high = lax.ppermute(lax.slice_in_dim(block, 0, width, axis=dim), axis, backward)
        block = jnp.concatenate([low, block, high], axis=dim)
    return block


def spread_rows(source, weights):
    rows_dev = source.shape[1]
    width_dev = source.shape[2]
    padded = padded_2(source, (("rows", 1),), 3)
    padded = jnp.pad(padded, ((0, 0), (0, 0), (3, 3), (0, 0))).astype(jnp.float32)
    running = jnp.zeros(source.shape, jnp.float32)
    for across in range(7):
        for along in range(7):
            running = (
                running
                + weights[across * 7 + along]
                * padded[:, across : across + rows_dev, along : along + width_dev]
            )
    return running


def local(activations, cotangent, proj_weight, kernel_taps, ln_gain, ln_shift, heights, widths):
    rows_dev = activations.shape[1]
    width_dev = activations.shape[2]
    chans = activations.shape[3]
    height_all = cotangent.shape[1]
    hidden_dev = cotangent.shape[3]
    offset_rows = lax.axis_index("rows") * rows_dev
    row_ids = lax.broadcasted_iota(jnp.int32, (height_all, width_dev), 0)
    col_ids = lax.broadcasted_iota(jnp.int32, (height_all, width_dev), 1)
    full_valid = ((row_ids < heights[0]) & (col_ids < widths[0])).astype(jnp.float32)
    own_valid = lax.dynamic_slice_in_dim(full_valid, offset_rows, rows_dev, 0)[None, :, :, None]
    weights = kernel_taps.astype(jnp.float32)
    masked = (activations.astype(jnp.float32) * own_valid).astype(jnp.bfloat16)
    mixed = spread_rows(masked, weights)
    centre = jnp.mean(mixed, axis=-1, keepdims=True)
    variance = jnp.mean((mixed - centre) ** 2, axis=-1, keepdims=True)
    inv_spread = 1.0 / jnp.sqrt(variance + epsilon)
    unit = (mixed - centre) * inv_spread
    normed = (unit * ln_gain + ln_shift).astype(jnp.bfloat16)
    normed_flat = normed.reshape(-1, chans)
    live_grad = (cotangent.astype(jnp.float32) * full_valid[None, :, :, None]).astype(jnp.bfloat16)
    grad_flat = live_grad.reshape(-1, hidden_dev)
    partial_value = lax.dot_general(
        lax.all_gather(normed_flat, "rows", axis=0, tiled=True),
        grad_flat,
        (((0,), (0,)), ((), ())),
        preferred_element_type=jnp.float32,
    )
    image_count = lax.axis_size("section") * activations.shape[0]
    weight_grad = (
        lax.psum_scatter(partial_value, "section", scatter_dimension=0, tiled=True) / image_count
    )
    proj_rows = lax.all_gather(proj_weight, "section", axis=0, tiled=True)
    own_grad = lax.all_to_all(live_grad, "rows", split_axis=1, concat_axis=3, tiled=True)
    proj_all = lax.all_gather(proj_rows, "rows", axis=1, tiled=True)
    own_flat = own_grad.reshape(-1, own_grad.shape[3])
    grad_norm = lax.dot_general(
        own_flat, proj_all, (((1,), (1,)), ((), ())), preferred_element_type=jnp.float32
    )
    grad_norm = grad_norm.reshape(mixed.shape)
    scaled = grad_norm * ln_gain
    grad_mixed = inv_spread * (
        scaled
        - jnp.mean(scaled, axis=-1, keepdims=True)
        - unit * jnp.mean(scaled * unit, axis=-1, keepdims=True)
    )
    grad_mixed = grad_mixed.astype(jnp.bfloat16)
    back = spread_rows(grad_mixed, weights[::-1]) * own_valid
    return (back.astype(jnp.bfloat16), weight_grad)


def solution(mesh):
    in_specs = (
        P("section", "rows", None, None),
        P("section", None, None, "rows"),
        P("section", "rows"),
        P(),
        P(),
        P(),
        P("section"),
        P("section"),
    )
    out_specs = (P("section", "rows", None, None), P("section", "rows"))
    return jax.shard_map(local, mesh=mesh, in_specs=in_specs, out_specs=out_specs, check_vma=False)
```

profile of v0, /device:TPU:6, one launch (start us, length us, event | category | flops | bytes accessed | tf_op | source)
XLA Modules:
  0.0 477.5 jit_solution(14129150594091430435)
XLA Ops:
  7.2 0.0 copy-start.1
  7.2 0.0 copy-start
  7.2 0.0 all-gather.3.cloned.1.call-start
  7.2 59.2 %all_gather.9 = bf16[768,192]{1,0:T(8,128)(2,1)S(1)} all-gather(bf16[16,192]{1,0:T(8,128)(2,1)} %param.10), channel_id=1, replica_groups=mesh['section'=48,'rows'=16] {'section'}, dimensions={0}, use_global_device_ids=true | all-gather | bytes 301056 | tf_op jit(solution)/shard_map/all_gather | solution.py:70
  66.4 0.9 copy.14
  67.3 0.0 all-gather.3.cloned.1.call-update
  68.6 0.1 and_convert_fusion
  68.7 0.0 copy-done.1
  68.7 0.1 multiply_convert_fusion.1
  68.9 4.0 collective-permute-start
  72.9 3.3 collective-permute-start.1
  76.2 0.0 copy-done
  76.2 1.4 multiply_convert_fusion
  77.6 10.5 %all-to-all-start = ((bf16[1,64,32,192]{3,2,0,1:T(8,128)(2,1)}), bf16[1,64,32,192]{3,2,0,1:T(8,128)(2,1)S(1)}, u32[]{:S(2)}, u32[]{:S(2)}) async-start(bf16[1,64,32,192]{3,2,0,1:T(8,128)(2,1)} %multiply_convert_fusion), calls=%async_computation | async-start | bytes 2097152 | tf_op jit(solution)/shard_map/all_to_all | solution.py:71
  88.1 0.0 all-gather.5.cloned.1.call-start
  88.1 0.0 copy-done.2
  88.2 0.2 slice_reduce_fusion.47
  88.3 0.1 slice_reduce_fusion.46
  88.4 0.2 slice_reduce_fusion.48
  88.6 0.0 collective-permute-done
  88.6 0.0 collective-permute-done.1
  88.6 0.2 fusion.12
  88.8 4.2 fusion.114
  93.0 0.2 multiply_reduce_fusion
  93.2 29.7 %all-to-all-done = bf16[1,64,32,192]{3,2,0,1:T(8,128)(2,1)S(1)} async-done(((bf16[1,64,32,192]{3,2,0,1:T(8,128)(2,1)}), bf16[1,64,32,192]{3,2,0,1:T(8,128)(2,1)S(1)}, u32[]{:S(2)}, u32[]{:S(2)}) %all-to-all-start) | async-done | bytes 786464 | tf_op jit(solution)/shard_map/all_to_all | solution.py:71
  122.9 0.6 copy.16
  123.5 0.0 copy-start.3
  123.5 0.0 copy-start.4
  123.6 1.1 dot_general.8
  124.7 59.8 %all-gather.3.cloned.1.call-done = bf16[768,3072]{0,1:T(8,128)(2,1)} async-done(((bf16[768,192]{0,1:T(8,128)(2,1)}), bf16[768,3072]{0,1:T(8,128)(2,1)}) %all-gather.3.cloned.1.call-update) | async-done | bytes 4718608 | tf_op jit(solution)/shard_map/all_gather | solution.py:72
  184.5 0.0 copy-done.3
  184.5 0.0 copy-done.4
  184.5 3.8 add_convert_fusion
  188.3 0.0 all-gather.5.cloned.1.call-update
  188.3 0.0 reduce-scatter.2.cloned.1.call-start
  188.3 0.1 reduce_sum.38
  188.5 0.2 fusion.113
  188.6 100.8 %all-gather.5.cloned.1.call-done = bf16[2048,768]{1,0:T(8,128)(2,1)} async-done(((bf16[128,768]{1,0:T(8,128)(2,1)}), bf16[2048,768]{1,0:T(8,128)(2,1)}) %all-gather.5.cloned.1.call-update) | async-done | bytes 3145744 | tf_op jit(solution)/shard_map/all_gather | solution.py:61
  289.4 4.1 fusion.118
  293.5 0.0 reduce-scatter.2.cloned.1.call-update
  293.5 4.7 collective-permute-start.2
  298.3 2.6 collective-permute-start.3
  300.9 2.8 collective-permute-done.2
  303.7 4.0 collective-permute-done.3
  307.7 0.2 fusion.6
  307.9 3.6 fusion.15
  311.4 158.2 %reduce-scatter.2.cloned.1.call-done = f32[16,192]{1,0:T(8,128)} async-done(((f32[768,192]{1,0:T(8,128)}), f32[16,192]{1,0:T(8,128)}) %reduce-scatter.2.cloned.1.call-update) | async-done | bytes 12304 | tf_op jit(solution)/shard_map/reduce_scatter | solution.py:68
  469.6 1.3 broadcast_multiply_fusion
  (11 shorter events, 0.1 us)
Async XLA Ops:
  7.2 61.6 %copy-start.1 = (bf16[1,4,32,768]{3,2,1,0:T(8,128)(2,1)S(1)}, bf16[1,4,32,768]{3,2,1,0:T(8,128)(2,1)}, u32[]{:S(2)}) copy-start(bf16[1,4,32,768]{3,2,1,0:T(8,128)(2,1)} %param.8) | copy-start | bytes 589828
  7.2 69.1 %copy-start = (bf16[1,64,32,192]{3,2,1,0:T(8,128)(2,1)S(1)}, bf16[1,64,32,192]{3,2,1,0:T(8,128)(2,1)}, u32[]{:S(2)}) copy-start(bf16[1,64,32,192]{3,2,1,0:T(8,128)(2,1)} %param.9) | copy-start | bytes 2359300
  7.2 177.3 %all-gather.3.cloned.1.call-start = ((), (), s32[]{:S(2)}) async-start(), calls=%async_computation.2 | async-start | bytes 5013504 | tf_op jit(solution)/shard_map/all_gather | solution.py:72
  68.9 19.7 %collective-permute-start = (bf16[1,3,32,768]{3,2,1,0:T(8,128)(2,1)S(1)}, bf16[1,3,32,768]{3,2,1,0:T(8,128)(2,1)S(1)}, u32[]{:S(2)}, u32[]{:S(2)}) collective-permute-start(bf16[1,3,32,768]{3,2,1,0:T(8,128)(2,1)S(1)} %get-tuple-element.57), channel_id=1, source_target_pairs={{0,1},{1,2},{2,3},{3,4},{4,5},{5,6},{6,7},{7,8},{8,9},{9,10},{10,1... | collective-permute-start | bytes 442376 | tf_op jit(solution)/shard_map/ppermute | solution.py:14
  72.9 15.7 %collective-permute-start.1 = (bf16[1,3,32,768]{3,2,1,0:T(8,128)(2,1)S(1)}, bf16[1,3,32,768]{3,2,1,0:T(8,128)(2,1)S(1)}, u32[]{:S(2)}, u32[]{:S(2)}) collective-permute-start(bf16[1,3,32,768]{3,2,1,0:T(8,128)(2,1)S(1)} %get-tuple-element.58), channel_id=1, source_target_pairs={{1,0},{2,1},{3,2},{4,3},{5,4},{6,5},{7,6},{8,7},{9,8},{10,9},{11,1... | collective-permute-start | bytes 442376 | tf_op jit(solution)/shard_map/ppermute | solution.py:17
  77.6 10.5 %copy-start.2 = (bf16[49,768]{1,0:T(8,128)(2,1)S(1)}, bf16[49,768]{1,0:T(8,128)(2,1)}, u32[]{:S(2)}) copy-start(bf16[49,768]{1,0:T(8,128)(2,1)} %param.11) | copy-start | bytes 225796
  77.6 45.3 %all-to-all-start = ((bf16[1,64,32,192]{3,2,0,1:T(8,128)(2,1)}), bf16[1,64,32,192]{3,2,0,1:T(8,128)(2,1)S(1)}, u32[]{:S(2)}, u32[]{:S(2)}) async-start(bf16[1,64,32,192]{3,2,0,1:T(8,128)(2,1)} %multiply_convert_fusion), calls=%async_computation | async-start | bytes 2097152 | tf_op jit(solution)/shard_map/all_to_all | solution.py:71
  88.1 201.3 %all-gather.5.cloned.1.call-start = ((), (), s32[]{:S(2)}) async-start(), calls=%async_computation.3 | async-start | bytes 3342336 | tf_op jit(solution)/shard_map/all_gather | solution.py:61
  123.5 61.0 %copy-start.3 = (f32[768]{0:T(1024)S(1)}, f32[768]{0:T(1024)}, u32[]{:S(2)}) copy-start(f32[768]{0:T(1024)} %param.12) | copy-start | bytes 9220
  123.5 61.0 %copy-start.4 = (f32[768]{0:T(1024)S(1)}, f32[768]{0:T(1024)}, u32[]{:S(2)}) copy-start(f32[768]{0:T(1024)} %param.13) | copy-start | bytes 9220
  188.3 281.3 %reduce-scatter.2.cloned.1.call-start = ((), (), s32[]{:S(2)}) async-start(), calls=%async_computation.4 | async-start | bytes 802816 | tf_op jit(solution)/shard_map/reduce_scatter | solution.py:68
  293.5 10.1 %collective-permute-start.2 = (bf16[1,3,32,768]{3,2,1,0:T(8,128)(2,1)S(1)}, bf16[1,3,32,768]{3,2,1,0:T(8,128)(2,1)S(1)}, u32[]{:S(2)}, u32[]{:S(2)}) collective-permute-start(bf16[1,3,32,768]{3,2,1,0:T(8,128)(2,1)S(1)} %get-tuple-element.55), channel_id=1, source_target_pairs={{0,1},{1,2},{2,3},{3,4},{4,5},{5,6},{6,7},{7,8},{8,9},{9,10},{10,1... | collective-permute-start | bytes 442376 | tf_op jit(solution)/shard_map/ppermute | solution.py:14
  298.3 9.4 %collective-permute-start.3 = (bf16[1,3,32,768]{3,2,1,0:T(8,128)(2,1)S(1)}, bf16[1,3,32,768]{3,2,1,0:T(8,128)(2,1)S(1)}, u32[]{:S(2)}, u32[]{:S(2)}) collective-permute-start(bf16[1,3,32,768]{3,2,1,0:T(8,128)(2,1)S(1)} %get-tuple-element.56), channel_id=1, source_target_pairs={{1,0},{2,1},{3,2},{4,3},{5,4},{6,5},{7,6},{8,7},{9,8},{10,9},{11,1... | collective-permute-start | bytes 442376 | tf_op jit(solution)/shard_map/ppermute | solution.py:17
Sparse Core Ops, SparseCore 0:
  67.4 117.0 all-gather.2
  188.8 100.5 all-gather.4
  293.6 175.9 reduce-scatter.1
where the time goes:
time: 478 us; the launch traced here: 477 us
  waiting for transfers between devices  355 us (74%)
  blocking collectives  59.2 us (12%)
  starting transfers between devices  25.3 us (5%)
  between operations  15.3 us (3%)
  other arithmetic  11.4 us (2%)
  matrix products  7.82 us (2%)
    reduce_scatter x1, waiting for transfers between devices, local(): lax.psum_scatter(partial_value, 'section', scatter_dimension=0, tiled=True)  158 us
    all_gather x1, waiting for transfers between devices, local(): lax.all_gather(normed_flat, 'rows', axis=0, tiled=True)  101 us
    all_gather x1, waiting for transfers between devices, local(): proj_all = lax.all_gather(proj_rows, 'rows', axis=1, tiled=True)  59.8 us
    all_gather x1, blocking collectives, local(): proj_rows = lax.all_gather(proj_weight, 'section', axis=0, tiled=True)  59.2 us
    all_to_all x1, waiting for transfers between devices, local(): lax.all_to_all(live_grad, 'rows', split_axis=1, concat_axis=3, tiled=True)  29.7 us
    all_to_all x1, starting transfers between devices, local(): lax.all_to_all(live_grad, 'rows', split_axis=1, concat_axis=3, tiled=True)  10.5 us
  transfers between devices with their start and end apart: 8, of which 6 were waited for; matrix products, arithmetic and copies ran while one was open for 3% of the time, Pallas kernels for 0%

commit v1 on v0

v1 whole, which is shorter than its diff:
```python
import functools

import jax
import jax.numpy as jnp
from jax import lax
from jax.experimental import pallas as pl
from jax.experimental.pallas import tpu as pltpu
from jax.sharding import PartitionSpec as P

EPS = 1e-06
BF = jnp.bfloat16
F32 = jnp.float32
LANE = 128


class Slots:
    def __init__(self):
        self.count = 0

    def take(self, n=1):
        first = self.count
        self.count += n
        return first


def kernel_body(
    ny, nz, images,
    h_ref, w_ref, act, g_a, g_b, wq, taps, gain, shift,
    ig, wg,
    actx, xp, tf, mx, inv, nrm, gm, gb, ws1, wall, wgp, r1, sp, sm, rp, rm,
    tot, r3, f4, r4, gnp, gns, gnr, gmx, ssem, rsem, lsem,
):
    s = lax.axis_index("section")
    r = lax.axis_index("rows")
    core = lax.rem(s, 2)
    z = lax.rem(lax.div(s, 2), nz)
    xl = lax.div(s, 2 * nz)
    y = lax.div(r, 2)
    xh = lax.rem(r, 2)
    width, chans = act.shape[1], act.shape[2]
    chunks = chans // LANE
    height_all = 8 * ny
    plus, minus = (nz - 1) // 2, nz // 2

    def sec(xl_, z_, c_):
        return (xl_ * nz + z_) * 2 + c_

    def yat(k):
        return lax.rem(y + k + ny, ny)

    def zat(k):
        return lax.rem(z + k + 2 * nz, nz)

    def row(y_, xh_):
        return y_ * 2 + xh_

    slots = Slots()
    started = []

    def send(src, dst, recv, s_, r_, ssem_id=None):
        sid = slots.take()
        cp = pltpu.make_async_remote_copy(
            src_ref=src, dst_ref=dst, send_sem=ssem.at[sid], recv_sem=rsem.at[recv],
            device_id={"section": s_, "rows": r_}, device_id_type=pl.DeviceIdType.MESH,
        )
        cp.start()
        started.append(cp)
        return cp

    recvs = Slots()
    core_s = sec(xl, z, 1 - core)
    xlp_s = sec(1 - xl, z, core)
    zp_s = sec(xl, zat(1), core)
    zm_s = sec(xl, zat(-1), core)

    barrier = pltpu.get_barrier_semaphore()
    peers = [(s, row(yat(k), xh)) for k in range(1, ny)]
    peers += [(s, row(y, 1 - xh)), (s, row(yat(1), 1 - xh)), (s, row(yat(-1), 1 - xh))]
    peers += [(core_s, r), (xlp_s, r), (zp_s, r), (zm_s, r)]
    for s_, r_ in peers:
        pl.semaphore_signal(
            barrier, inc=1, device_id={"section": s_, "rows": r_},
            device_id_type=pl.DeviceIdType.MESH,
        )
    pl.semaphore_wait(barrier, len(peers))

    a_pair, a_halo = recvs.take(), recvs.take(2)
    act_cp = [send(act, actx.at[pl.ds(3 + 4 * xh, 4)], a_pair, s, row(y, 1 - xh))]
    halo_y = yat(2 * xh - 1)
    for to in range(2):
        act_cp.append(
            send(act.at[pl.ds(xh, 3)], actx.at[pl.ds(11 * (1 - xh), 3)], a_halo + xh, s, row(halo_y, to))
        )
    own_act = pltpu.make_async_copy(act, actx.at[pl.ds(3 + 4 * xh, 4)], lsem.at[0])
    own_act.start()

    w1 = recvs.take(ny)
    w1_cp = [send(wq, ws1.at[y], w1 + k, s, row(yat(k), xh)) for k in range(1, ny)]

    ga_id, gb_id = recvs.take(ny), recvs.take(ny)
    g_cp = []
    order = sorted(range(1, ny), key=lambda k: -min(k, ny - k))
    for k in order:
        g_cp.append(send(g_a.at[yat(k)], gm.at[y], ga_id + k, s, row(yat(k), xh)))
        g_cp.append(send(g_b.at[yat(k)], gb.at[y], gb_id + k, s, row(yat(k), xh)))
    own_ga = pltpu.make_async_copy(g_a.at[y], gm.at[y], lsem.at[1])
    own_gb = pltpu.make_async_copy(g_b.at[y], gb.at[y], lsem.at[2])
    own_ga.start()
    own_gb.start()

    ws1[y] = wq[...]
    tf[pl.ds(0, 49), :] = taps[...].astype(F32)
    xp[...] = jnp.zeros_like(xp)

    for cp in w1_cp:
        cp.wait_recv()
    for k in range(ny):
        wall[s, :, k * LANE:(k + 1) * LANE] = ws1[k, :, 0:LANE]
    for k in range(ny // 2):
        wall[s, :, (ny + k) * LANE:(ny + k + 1) * LANE] = ws1[2 * k, :, LANE:] + ws1[2 * k + 1, :, LANE:]

    w2 = recvs.take()
    wp_id, wm_id, wc_id = recvs.take(2 * plus), recvs.take(2 * minus), recvs.take(2 * nz)
    wc_cp = []

    def wblock(sub, z_):
        xl_ = xl if sub == 0 else 1 - xl
        return wall.at[sec(xl_, z_, core)]

    def to_core(sub, z_):
        blk = wblock(sub, z_)
        wc_cp.append(send(blk, blk, wc_id + len(wc_cp), core_s, r))

    wp_cp, wm_cp = {}, {}

    def ring_w(t, sub):
        if t < plus:
            blk = wblock(sub, zat(-t))
            wp_cp[t, sub] = send(blk, blk, wp_id + 2 * t + sub, zp_s, r)
        if t < minus:
            blk = wblock(sub, zat(t))
            wm_cp[t, sub] = send(blk, blk, wm_id + 2 * t + sub, zm_s, r)

    ring_w(0, 0)
    x2 = send(wall.at[s], wall.at[s], w2, xlp_s, r)
    to_core(0, z)

    def ring_w_open():
        x2.wait_recv()
        ring_w(0, 1)
        to_core(1, z)

    def ring_w_step(t):
        for sub in range(2):
            if t <= plus:
                wp_cp[t - 1, sub].wait_recv()
            wm_cp[t - 1, sub].wait_recv()
            ring_w(t, sub)
            if t <= plus:
                to_core(sub, zat(-t))
            to_core(sub, zat(t))

    height, wid = h_ref[0], w_ref[0]
    col_ids = lax.broadcasted_iota(jnp.int32, (width, chans), 0)

    def conv(base, rows_out, flip, lane, put):
        lanes = pl.ds(pl.multiple_of(lane * LANE, LANE), LANE)
        total = [None] * rows_out
        for along in range(7):
            taps_here = []
            for across in range(7):
                i = across * 7 + along
                taps_here.append(tf[pl.ds(48 - i if flip else i, 1), lanes])
            for rho in range(rows_out + 6):
                x = xp[base + rho, 5 + along:5 + along + width, lanes]
                for out in range(max(0, rho - 6), min(rows_out, rho + 1)):
                    term = taps_here[rho - out] * x
                    total[out] = term if total[out] is None else total[out] + term
        for out in range(rows_out):
            put(out, lanes, total[out])

    for cp in act_cp[:1]:
        cp.wait_recv()
    for i in range(2):
        pltpu.make_async_remote_copy(
            src_ref=act.at[pl.ds(xh, 3)], dst_ref=actx.at[pl.ds(11 * (1 - i), 3)],
            send_sem=ssem.at[0], recv_sem=rsem.at[a_halo + i],
            device_id={"section": s, "rows": row(halo_y, 0)}, device_id_type=pl.DeviceIdType.MESH,
        ).wait_recv()
    own_act.wait()

    def expand(i, carry):
        line = 8 * y - 3 + i
        ok = (col_ids < wid) & (line >= 0) & (line < height)
        xp[i, 8:8 + width, :] = jnp.where(ok, actx[i].astype(F32), 0.0)
        return carry

    lax.fori_loop(0, 14, expand, 0)

    ring_w_open()

    def put_mixed(out, lanes, value):
        mx[pl.ds(out * width, width), lanes] = value

    def conv_fwd(lane, carry):
        conv(0, 8, False, lane, put_mixed)
        return carry

    lax.fori_loop(0, chunks // 2, conv_fwd, 0)
    ring_w_step(1)
    lax.fori_loop(chunks // 2, chunks, conv_fwd, 0)
    ring_w_step(2)

    def norm(i, carry):
        px = pl.ds(pl.multiple_of(i * width, width), width)
        x = mx[px, :]
        centre = jnp.mean(x, axis=-1, keepdims=True)
        dev = x - centre
        inv_spread = 1.0 / jnp.sqrt(jnp.mean(dev * dev, axis=-1, keepdims=True) + EPS)
        unit = dev * inv_spread
        mx[px, :] = unit
        inv[px, :] = jnp.broadcast_to(inv_spread, (width, LANE))
        nrm[px, :] = (unit * gain[...] + shift[...]).astype(BF)
        return carry

    lax.fori_loop(0, 8, norm, 0)
    for t in range(3, minus + 1):
        ring_w_step(t)

    for cp in g_cp:
        cp.wait_recv()
    own_ga.wait()
    own_gb.wait()
    half = gb.shape[1]
    low = lax.broadcasted_iota(jnp.int32, (half, LANE), 1) < LANE // 2
    for k in range(ny // 2):
        even, odd = gb[2 * k].astype(F32), gb[2 * k + 1].astype(F32)
        gm[ny + k, 0:half, :] = jnp.where(low, even, pltpu.roll(odd, LANE // 2, 1)).astype(BF)
        gm[ny + k, half:2 * half, :] = jnp.where(low, pltpu.roll(even, LANE // 2, 1), odd).astype(BF)

    blocks = gm.shape[0]

    def weight_part(j, carry):
        g2 = jnp.concatenate([gm[2 * j], gm[2 * j + 1]], axis=1)
        lanes = pl.ds(pl.multiple_of(j * 2 * LANE, 2 * LANE), 2 * LANE)
        for i in range(chans // 256):
            part = lax.dot_general(
                nrm[:, i * 256:(i + 1) * 256], g2, (((0,), (0,)), ((), ())), preferred_element_type=F32
            )
            wgp[8 * i:8 * i + 8, :, :, lanes] = part.astype(BF).reshape(8, 2, 16, 2 * LANE)
        return carry

    lax.fori_loop(0, blocks // 2, weight_part, 0)
    r1_id = recvs.take()
    r1_cp = send(wgp.at[:, 1 - core], r1, r1_id, core_s, r)

    for cp in wc_cp:
        cp.wait_recv()

    def grad_part(i, carry):
        here = wall[pl.ds(i * 16, 16)].reshape(256, blocks * LANE)
        value = jnp.zeros((gm.shape[1], 256), F32)
        for j in range(blocks // 2):
            g2 = jnp.concatenate([gm[2 * j], gm[2 * j + 1]], axis=1)
            value = value + lax.dot_general(
                g2, here[:, j * 256:(j + 1) * 256], (((1,), (1,)), ((), ())), preferred_element_type=F32
            )
        lanes = pl.ds(pl.multiple_of(i * 256, 256), 256)
        gnp[:, lanes] = value
        gns[:, lanes] = value.astype(BF)
        return carry

    lax.fori_loop(0, chans // 256, grad_part, 0)
    gn_id = recvs.take()
    gn_cp = send(gns, gnr, gn_id, s, row(y, 1 - xh))

    r1_cp.wait_recv()
    rp_id, rm_id = recvs.take(2 * plus), recvs.take(2 * minus)

    def local_sum(sub, z_):
        at = sub * nz + z_
        return wgp[at, core].astype(F32) + r1[at].astype(F32)

    rp_cp, rm_cp = {}, {}

    def ring_r(t):
        for sub in range(2):
            if t < minus:
                value = local_sum(sub, zat(t - minus))
                if t > 0:
                    rm_cp[t - 1, sub].wait_recv()
                    value = value + rm[t - 1, sub].astype(F32)
                sm[t, sub] = value.astype(BF)
                rm_cp[t, sub] = send(sm.at[t, sub], rm.at[t, sub], rm_id + 2 * t + sub, zm_s, r)
            if t < plus:
                value = local_sum(sub, zat(plus - t))
                if t > 0:
                    rp_cp[t - 1, sub].wait_recv()
                    value = value + rp[t - 1, sub].astype(F32)
                sp[t, sub] = value.astype(BF)
                rp_cp[t, sub] = send(sp.at[t, sub], rp.at[t, sub], rp_id + 2 * t + sub, zp_s, r)

    ring_r(0)
    ring_r(1)

    gn_cp.wait_recv()

    def norm_back(i, carry):
        px = pl.ds(pl.multiple_of(i * width, width), width)
        scaled = (gnp[px, :] + gnr[px, :].astype(F32)) * gain[...]
        unit = mx[px, :]
        first = jnp.mean(scaled, axis=-1, keepdims=True)
        second = jnp.mean(scaled * unit, axis=-1, keepdims=True)
        gmx[3 + i] = (inv[px, 0:1] * (scaled - first - unit * second)).astype(BF)
        return carry

    lax.fori_loop(0, 8, norm_back, 0)
    hb_id = recvs.take()
    hb_cp = send(
        gmx.at[pl.ds(8 - 5 * xh, 3)], gmx.at[pl.ds(11 * xh, 3)], hb_id, s, row(yat(1 - 2 * xh), xh)
    )
    ring_r(2)
    hb_cp.wait_recv()

    def expand_back(i, carry):
        at = 4 * xh + i
        line = 8 * y - 3 + at
        ok = (line >= 0) & (line < height_all) & (col_ids >= 0)
        xp[i, 8:8 + width, :] = jnp.where(ok, gmx[at].astype(F32), 0.0)
        return carry

    lax.fori_loop(0, 10, expand_back, 0)
    out_cols = lax.broadcasted_iota(jnp.int32, (width, LANE), 0)

    def put_out(out, lanes, value):
        ok = (out_cols < wid) & (8 * y + 4 * xh + out < height)
        ig[out, :, lanes] = jnp.where(ok, value, 0.0).astype(BF)

    def conv_back(lane, carry):
        conv(0, 4, True, lane, put_out)
        return carry

    lax.fori_loop(0, chunks // 2, conv_back, 0)
    ring_r(3)
    lax.fori_loop(chunks // 2, chunks, conv_back, 0)
    for t in range(4, minus):
        ring_r(t)
    for sub in range(2):
        rm_cp[minus - 1, sub].wait_recv()
        rp_cp[plus - 1, sub].wait_recv()
        tot[sub] = local_sum(sub, z) + rm[minus - 1, sub].astype(F32) + rp[plus - 1, sub].astype(F32)

    r3_id = recvs.take()
    r3_cp = send(tot.at[1 - xl], r3, r3_id, xlp_s, r)
    r3_cp.wait_recv()
    done = tot[xl] + r3[...]
    for k in range(ny):
        f4[k, 0] = done[:, k * LANE:(k + 1) * LANE]
        at = ny + k // 2
        f4[k, 1] = done[:, at * LANE:(at + 1) * LANE]
    r4_id = recvs.take(ny)
    r4_cp = [send(f4.at[yat(k)], r4.at[y], r4_id + k, s, row(yat(k), xh)) for k in range(1, ny)]
    for cp in r4_cp:
        cp.wait_recv()
    r4[y] = f4[y]
    total = r4[0]
    for k in range(1, ny):
        total = total + r4[k]
    tail = jnp.where(lax.rem(y, 2) == 0, total[1], pltpu.roll(total[1], LANE // 2, 1))
    wg[:, 0:LANE] = total[0] / images
    wg[:, LANE:] = tail[:, 0:LANE // 2] / images

    for cp in started:
        cp.wait_send()
    assert slots.count <= ssem.shape[0] and recvs.count <= rsem.shape[0]


def local(ny, nz, images, activations, cotangent, proj_weight, kernel_taps, ln_gain, ln_shift, heights, widths):
    rows_dev, width, chans = activations.shape[1:]
    height_all, hidden = cotangent.shape[1], cotangent.shape[3]
    blocks = ny + ny // 2
    px = 2 * rows_dev * width
    row_ids = lax.broadcasted_iota(jnp.int32, (height_all, width), 0)
    col_ids = lax.broadcasted_iota(jnp.int32, (height_all, width), 1)
    valid = (row_ids < heights[0]) & (col_ids < widths[0])
    live = jnp.where(valid[:, :, None], cotangent[0], jnp.zeros((), BF))
    g_a = live[:, :, :LANE].reshape(ny, px, LANE)
    tail = live[:, :, LANE:].reshape(ny, 2, px // 2, hidden - LANE)
    g_b = jnp.concatenate([tail[:, 0], tail[:, 1]], axis=-1)
    odd = lax.rem(lax.div(lax.axis_index("rows"), 2), 2) == 1
    w_tail = proj_weight[:, LANE:]
    w_none = jnp.zeros_like(w_tail)
    wq = jnp.concatenate(
        [proj_weight[:, :LANE], jnp.where(odd, w_none, w_tail), jnp.where(odd, w_tail, w_none)], axis=-1
    )
    plus, minus = (nz - 1) // 2, nz // 2
    cols = blocks * LANE
    vmem = pltpu.VMEM
    out = pl.pallas_call(
        functools.partial(kernel_body, ny, nz, float(images)),
        out_shape=(
            jax.ShapeDtypeStruct((rows_dev, width, chans), BF),
            jax.ShapeDtypeStruct((16, hidden), F32),
        ),
        in_specs=[pl.BlockSpec(memory_space=pltpu.SMEM)] * 2
        + [pl.BlockSpec(memory_space=pl.ANY)] * 3
        + [pl.BlockSpec(memory_space=vmem)] * 4,
        out_specs=[pl.BlockSpec(memory_space=vmem)] * 2,
        scratch_shapes=[
            vmem((14, width, chans), BF),
            vmem((14, width + 16, chans), F32),
            vmem((56, chans), F32),
            vmem((px, chans), F32),
            vmem((px, LANE), F32),
            vmem((px, chans), BF),
            vmem((blocks, px, LANE), BF),
            vmem((ny, px // 2, LANE), BF),
            vmem((ny, 16, 2 * LANE), BF),
            vmem((4 * nz, 16, cols), BF),
            vmem((2 * nz, 2, 16, cols), BF),
            vmem((2 * nz, 16, cols), BF),
            vmem((plus, 2, 16, cols), BF),
            vmem((minus, 2, 16, cols), BF),
            vmem((plus, 2, 16, cols), BF),
            vmem((minus, 2, 16, cols), BF),
            vmem((2, 16, cols), F32),
            vmem((16, cols), F32),
            vmem((ny, 2, 16, LANE), F32),
            vmem((ny, 2, 16, LANE), F32),
            vmem((px, chans), F32),
            vmem((px, chans), BF),
            vmem((px, chans), BF),
            vmem((14, width, chans), BF),
            pltpu.SemaphoreType.DMA((160,)),
            pltpu.SemaphoreType.DMA((160,)),
            pltpu.SemaphoreType.DMA((3,)),
        ],
        compiler_params=pltpu.CompilerParams(
            collective_id=0, has_side_effects=True, vmem_limit_bytes=60 * 1024 * 1024
        ),
    )(
        heights, widths, activations[0], g_a, g_b, wq, kernel_taps,
        ln_gain.reshape(1, chans), ln_shift.reshape(1, chans),
    )
    return out[0][None], out[1]


def solution(mesh):
    ny = mesh.shape["rows"] // 2
    nz = mesh.shape["section"] // 4
    in_specs = (
        P("section", "rows", None, None),
        P("section", None, None, "rows"),
        P("section", "rows"),
        P(),
        P(),
        P(),
        P("section"),
        P("section"),
    )
    out_specs = (P("section", "rows", None, None), P("section", "rows"))
    body = functools.partial(local, ny, nz, mesh.shape["section"])
    return jax.shard_map(body, mesh=mesh, in_specs=in_specs, out_specs=out_specs, check_vma=False)
```

time: 478 us -> 114 us (0.24)
  waiting for transfers between devices: 355 us -> 0 us
  Pallas kernels: 0 us -> 102 us
  blocking collectives: 59.2 us -> 0 us
  starting transfers between devices: 25.3 us -> 0 us
  between operations: 15.3 us -> 1.98 us
  other arithmetic: 11.4 us -> 3.11 us
  matrix products: 7.82 us -> 0 us
    all_gather x2 -> x0, waiting for transfers between devices: 161 us -> none  [the longest x1 101 us: local(): lax.all_gather(normed_flat, 'rows', axis=0, tiled=True)]
    reduce_scatter x1 -> x0, waiting for transfers between devices: 158 us -> none  [local(): lax.psum_scatter(partial_value, 'section', scatter_dimension=0, tiled=True)]
    pallas_call x0 -> x1, Pallas kernels: none -> 102 us  [local(): pl.pallas_call(functools.partial(kernel_body, ny, nz, float(images)), out...]
    all_gather x1 -> x0, blocking collectives: 59.2 us -> none  [local(): proj_rows = lax.all_gather(proj_weight, 'section', axis=0, tiled=True)]
    all_to_all x1 -> x0, waiting for transfers between devices: 29.7 us -> none  [local(): lax.all_to_all(live_grad, 'rows', split_axis=1, concat_axis=3, tiled=True)]
    ppermute x4 -> x0, starting transfers between devices: 14.7 us -> none  [the longest x2 8.75 us: padded_2(): lax.ppermute(lax.slice_in_dim(block, block.shape[dim] - width, None, axis...]
    all_to_all x1 -> x0, starting transfers between devices: 10.5 us -> none  [local(): lax.all_to_all(live_grad, 'rows', split_axis=1, concat_axis=3, tiled=True)]
    dot_general x2 -> x0, matrix products: 7.82 us -> none  [the longest x1 4.07 us: local(): lax.dot_general(lax.all_gather(normed_flat, 'rows', axis=0, tiled=True),...]
  transfers between devices with their start and end apart: 8 -> 0, of which waited for: 6 -> 0; matrix products, arithmetic and copies ran while one was open for 3% -> 0% of each run, Pallas kernels for 0% -> 0%
where the time goes in v1:
time: 114 us; the launch traced here: 113 us
  Pallas kernels  102 us (89%)
  local copies, waits for them, and re-layouts  5.93 us (5%)
  other arithmetic  3.11 us (3%)
  between operations  1.98 us (2%)
    pallas_call x1, Pallas kernels, local(): pl.pallas_call(functools.partial(kernel_body, ny, nz, float(images)), out...  102 us
    unnamed x10, local copies, waits for them, and re-layouts  3.05 us

profile of v1, /device:TPU:6, one launch (start us, length us, event | category | flops | bytes accessed | tf_op | source)
XLA Modules:
  0.0 112.8 jit_solution(12532806895091286173)
XLA Ops:
  1.9 0.1 broadcast_and_fusion
  2.0 1.5 %bitcast_select_fusion = bf16[64,32,192]{2,1,0:T(8,128)(2,1)S(1)} fusion(bf16[1,64,32,192]{3,2,1,0:T(8,128)(2,1)} %param.9, pred[64,32]{1,0:T(8,128)(4,1)S(1)} %broadcast_and_fusion), kind=kLoop, calls=%fused_computation | loop fusion | flops 393216 | bytes 1574912 | tf_op jit(solution)/shard_map/jit(_where)/select_n | solution.py:386
  3.5 0.9 slice.24
  4.4 0.1 slice.25
  4.6 0.9 pad_maximum_fusion.g_b
  5.4 0.0 copy-start
  5.4 0.7 copy-done
  6.1 0.0 slice-start
  6.1 0.7 slice-done
  6.8 0.0 copy-start.2
  6.8 0.7 pad_maximum_fusion.1.wq
  7.5 0.0 copy-done.2
  7.5 0.0 copy-start.3
  7.5 0.6 reshape.41.gain
  8.1 0.1 copy-done.3
  8.2 0.6 reshape.42.shift
  8.8 101.8 %shard_map.95 = (bf16[4,32,768]{2,1,0:T(8,128)(2,1)}, f32[16,192]{1,0:T(8,128)}) custom-call(s32[1]{0:T(128)} %copy.16.h_ref, s32[1]{0:T(128)} %copy.17.w_ref, bf16[4,32,768]{2,1,0:T(8,128)(2,1)} %bitcast.20, bf16[8,256,128]{2,1,0:T(8,128)(2,1)} %bitcast.18, bf16[8,128,128]{2,1,0:T(8,128)(2,1)} %pad_maximum_fusion.g_b, ...), custom_call_target="tpu_custom_call" | custom-call | tf_op jit(solution)/shard_map/pallas_call | solution.py:399
  110.5 0.0 copy-start.1
  110.5 1.6 %copy.18 = bf16[1,4,32,768]{3,2,1,0:T(8,128)(2,1)} copy(bf16[1,4,32,768]{3,2,1,0:T(8,128)(2,1)} %bitcast.21) | data formatting | bytes 393216
  112.2 0.0 copy-done.1
  112.2 0.6 copy.19
  (4 shorter events, 0.1 us)
Async XLA Ops:
  5.4 0.7 copy-start
  6.1 0.7 slice-start
  6.8 0.7 copy-start.2
  7.5 0.7 copy-start.3
  110.5 1.6 %copy-start.1 = (f32[16,192]{1,0:T(8,128)S(1)}, f32[16,192]{1,0:T(8,128)}, u32[]{:S(2)}) copy-start(f32[16,192]{1,0:T(8,128)} %get-tuple-element.13) | copy-start | bytes 36868

commit v2 on v1

v2 whole, which is shorter than its diff:
```python
import functools

import jax
import jax.numpy as jnp
from jax import lax
from jax.experimental import pallas as pl
from jax.experimental.pallas import tpu as pltpu
from jax.sharding import PartitionSpec as P

EPS = 1e-06
BF = jnp.bfloat16
F32 = jnp.float32
LANE = 128


class Slots:
    def __init__(self):
        self.count = 0

    def take(self, n=1):
        first = self.count
        self.count += n
        return first


def kernel_body(
    ny, nz, images,
    h_ref, w_ref, act, cot, proj, taps, gain, shift,
    ig, wg,
    actx, xp, tf, mx, inv, nrm, cbuf, g_a, g_b, gm, gb, wq, ws1, wall, wgp, r1, sp, sm, rp, rm,
    f4, r4, gnp, gns, gnr, gmx, ssem, rsem, lsem,
):
    s = lax.axis_index("section")
    r = lax.axis_index("rows")
    core = lax.rem(s, 2)
    z = lax.rem(lax.div(s, 2), nz)
    xl = lax.div(s, 2 * nz)
    y = lax.div(r, 2)
    xh = lax.rem(r, 2)
    width, chans = act.shape[1], act.shape[2]
    chunks = chans // LANE
    height_all = cot.shape[0]
    half_px = g_b.shape[1]
    plus, minus = (nz - 1) // 2, nz // 2
    quarter = ny // 2
    per_half = quarter + quarter // 2
    blocks = 2 * per_half
    off = sorted(range(ny), key=lambda k: min(k, ny - k))

    def main_block(p):
        return per_half * (p // quarter) + p % quarter

    def pair_block(p):
        return per_half * (p // quarter) + quarter + (p % quarter) // 2

    def sec(xl_, z_, c_):
        return (xl_ * nz + z_) * 2 + c_

    def yat(k):
        return lax.rem(y + k + ny, ny)

    def zat(k):
        return lax.rem(z + k + 2 * nz, nz)

    def row(y_, xh_):
        return y_ * 2 + xh_

    def lanes_of(i, n=1):
        return slice(i * LANE, (i + n) * LANE)

    slots = Slots()
    recvs = Slots()
    started = []

    def send(src, dst, recv, s_, r_):
        cp = pltpu.make_async_remote_copy(
            src_ref=src, dst_ref=dst, send_sem=ssem.at[slots.take()], recv_sem=rsem.at[recv],
            device_id={"section": s_, "rows": r_}, device_id_type=pl.DeviceIdType.MESH,
        )
        cp.start()
        started.append(cp)
        return cp

    core_s = sec(xl, z, 1 - core)
    xlp_s = sec(1 - xl, z, core)
    zp_s = sec(xl, zat(1), core)
    zm_s = sec(xl, zat(-1), core)

    barrier = pltpu.get_barrier_semaphore()
    peers = [(xs, row(yat(k), xh)) for k in range(ny) for xs in (s, xlp_s) if not (k == 0 and xs is s)]
    peers += [(s, row(y, 1 - xh)), (s, row(yat(1), 1 - xh)), (s, row(yat(-1), 1 - xh))]
    peers += [(core_s, r), (zp_s, r), (zm_s, r)]
    for s_, r_ in peers:
        pl.semaphore_signal(
            barrier, inc=1, device_id={"section": s_, "rows": r_},
            device_id_type=pl.DeviceIdType.MESH,
        )

    own_cot = pltpu.make_async_copy(cot, cbuf, lsem.at[1])
    own_cot.start()
    own_act = pltpu.make_async_copy(act, actx.at[pl.ds(3 + 4 * xh, 4)], lsem.at[0])
    own_act.start()
    wq[:, LANE:] = jnp.zeros((16, LANE), BF)
    wq[:, 0:proj.shape[1]] = proj[...]
    ws1[0] = wq[...]
    tf[pl.ds(0, 49), :] = taps[...].astype(F32)
    xp[...] = jnp.zeros_like(xp)
    height, wid = h_ref[0], w_ref[0]
    own_cot.wait()
    cols3 = lax.broadcasted_iota(jnp.int32, (8, width, LANE), 1)
    rows3 = lax.broadcasted_iota(jnp.int32, (8, width, LANE), 0)
    low = lax.broadcasted_iota(jnp.int32, (half_px, LANE), 1) < LANE // 2

    def pack(i, carry):
        lines = pl.ds(pl.multiple_of(i * 8, 8), 8)
        ok = (cols3 < wid) & (rows3 + i * 8 < height)
        main = jnp.where(ok, cbuf[lines, :, 0:LANE].astype(F32), 0.0)
        g_a[i] = main.astype(BF).reshape(2 * half_px, LANE)
        tail = cbuf[lines, :, LANE:].astype(F32)
        tail = jnp.concatenate([tail, tail], axis=-1)
        tail = jnp.where(ok, tail, 0.0).reshape(2 * half_px, LANE)
        g_b[i] = jnp.where(low, tail[:half_px], tail[half_px:]).astype(BF)
        return carry

    lax.fori_loop(0, ny, pack, 0)
    pl.semaphore_wait(barrier, len(peers))

    w1 = recvs.take(2 * ny)
    w1_cp = []
    for p in range(ny):
        for sub in range(2):
            if p or sub:
                w1_cp.append(
                    send(wq, ws1.at[2 * p + sub], w1 + 2 * p + sub, xlp_s if sub else s, row(yat(-off[p]), xh))
                )

    a_pair, a_halo = recvs.take(), recvs.take(2)
    pair_cp = send(act, actx.at[pl.ds(3 + 4 * xh, 4)], a_pair, s, row(y, 1 - xh))
    halo_y = yat(2 * xh - 1)
    for to in range(2):
        halo_cp = send(
            act.at[pl.ds(xh, 3)], actx.at[pl.ds(11 * (1 - xh), 3)], a_halo + xh, s, row(halo_y, to)
        )

    ga_id, gb_id = recvs.take(ny), recvs.take(ny)
    g_cp = {}
    for p in range(1, ny):
        to = yat(-off[p])
        g_cp[p] = (
            send(g_a.at[to], gm.at[main_block(p)], ga_id + p, s, row(to, xh)),
            send(g_b.at[to], gb.at[p], gb_id + p, s, row(to, xh)),
        )
    own_ga = pltpu.make_async_copy(g_a.at[y], gm.at[0], lsem.at[1])
    own_gb = pltpu.make_async_copy(g_b.at[y], gb.at[0], lsem.at[2])
    own_ga.start()
    own_gb.start()

    wp_id, wm_id, wc_id = recvs.take(2 * plus), recvs.take(2 * minus), recvs.take(2 * nz)
    wc_cp = []
    wp_cp, wm_cp = {}, {}

    def wblock(sub, z_):
        return wall.at[sec(1 - xl if sub else xl, z_, core)]

    def to_core(sub, z_):
        blk = wblock(sub, z_)
        wc_cp.append(send(blk, blk, wc_id + len(wc_cp), core_s, r))

    def ring_w(t, sub):
        if t < plus:
            blk = wblock(sub, zat(-t))
            wp_cp[t, sub] = send(blk, blk, wp_id + 2 * t + sub, zp_s, r)
        if t < minus:
            blk = wblock(sub, zat(t))
            wm_cp[t, sub] = send(blk, blk, wm_id + 2 * t + sub, zm_s, r)

    low16 = lax.broadcasted_iota(jnp.int32, (16, LANE), 1) < LANE // 2

    def ring_w_open():
        for cp in w1_cp:
            cp.wait_recv()
        for sub in range(2):
            at = sec(1 - xl if sub else xl, z, core)
            for p in range(ny):
                wall[at, :, lanes_of(main_block(p))] = ws1[2 * p + sub, :, 0:LANE]
            for p in range(0, ny, 2):
                first = ws1[2 * p + sub, :, LANE:].astype(F32)
                second = ws1[2 * p + 2 + sub, :, LANE:].astype(F32)
                wall[at, :, lanes_of(pair_block(p))] = jnp.where(
                    low16, first, pltpu.roll(second, LANE // 2, 1)
                ).astype(BF)
        for sub in range(2):
            ring_w(0, sub)
        for sub in range(2):
            to_core(sub, z)

    def ring_w_step(t):
        for sub in range(2):
            if t <= plus:
                wp_cp[t - 1, sub].wait_recv()
            wm_cp[t - 1, sub].wait_recv()
            ring_w(t, sub)
            if t <= plus:
                to_core(sub, zat(-t))
            to_core(sub, zat(t))

    col_ids = lax.broadcasted_iota(jnp.int32, (width, chans), 0)

    def conv(rows_out, flip, lane, put):
        lanes = pl.ds(pl.multiple_of(lane * LANE, LANE), LANE)
        total = [None] * rows_out
        for along in range(7):
            taps_here = []
            for across in range(7):
                i = across * 7 + along
                taps_here.append(tf[pl.ds(48 - i if flip else i, 1), lanes])
            for rho in range(rows_out + 6):
                x = xp[rho, 5 + along:5 + along + width, lanes]
                for out in range(max(0, rho - 6), min(rows_out, rho + 1)):
                    term = taps_here[rho - out] * x
                    total[out] = term if total[out] is None else total[out] + term
        for out in range(rows_out):
            put(out, lanes, total[out])

    ring_w_open()
    ring_w_step(1)
    pair_cp.wait_recv()
    for i in range(2):
        pltpu.make_async_remote_copy(
            src_ref=act.at[pl.ds(xh, 3)], dst_ref=actx.at[pl.ds(11 * (1 - i), 3)],
            send_sem=ssem.at[0], recv_sem=rsem.at[a_halo + i],
            device_id={"section": s, "rows": row(halo_y, 0)}, device_id_type=pl.DeviceIdType.MESH,
        ).wait_recv()
    own_act.wait()

    def expand(i, carry):
        line = 8 * y - 3 + i
        ok = (col_ids < wid) & (line >= 0) & (line < height)
        xp[i, 8:8 + width, :] = jnp.where(ok, actx[i].astype(F32), 0.0)
        return carry

    lax.fori_loop(0, 14, expand, 0)

    def put_mixed(out, lanes, value):
        mx[pl.ds(out * width, width), lanes] = value

    def conv_fwd(lane, carry):
        conv(8, False, lane, put_mixed)
        return carry

    lax.fori_loop(0, chunks // 2, conv_fwd, 0)
    ring_w_step(2)
    lax.fori_loop(chunks // 2, chunks, conv_fwd, 0)
    ring_w_step(3)

    def norm(i, carry):
        px = pl.ds(pl.multiple_of(i * width, width), width)
        x = mx[px, :]
        centre = jnp.mean(x, axis=-1, keepdims=True)
        dev = x - centre
        inv_spread = 1.0 / jnp.sqrt(jnp.mean(dev * dev, axis=-1, keepdims=True) + EPS)
        unit = dev * inv_spread
        mx[px, :] = unit
        inv[px, :] = jnp.broadcast_to(inv_spread, (width, LANE))
        nrm[px, :] = (unit * gain[...] + shift[...]).astype(BF)
        return carry

    lax.fori_loop(0, 8, norm, 0)

    r1_id = recvs.take(2)
    r1_cp = {}

    def weight_half(h):
        for p in range(h * quarter, (h + 1) * quarter):
            if p:
                g_cp[p][0].wait_recv()
                g_cp[p][1].wait_recv()
        if h == 0:
            own_ga.wait()
            own_gb.wait()
        for p in range(h * quarter, (h + 1) * quarter, 2):
            first, second = gb[p].astype(F32), gb[p + 1].astype(F32)
            at = pair_block(p)
            gm[at, 0:half_px, :] = jnp.where(low, first, pltpu.roll(second, LANE // 2, 1)).astype(BF)
            gm[at, half_px:, :] = jnp.where(low, pltpu.roll(first, LANE // 2, 1), second).astype(BF)

        def weight_part(j, carry):
            at = h * per_half + 2 * j
            g2 = jnp.concatenate([gm[at], gm[at + 1]], axis=1)
            lanes = pl.ds(pl.multiple_of(j * 2 * LANE, 2 * LANE), 2 * LANE)
            for i in range(chans // 256):
                part = lax.dot_general(
                    nrm[:, i * 256:(i + 1) * 256], g2, (((0,), (0,)), ((), ())), preferred_element_type=F32
                )
                wgp[h, 8 * i:8 * i + 8, :, :, lanes] = part.astype(BF).reshape(8, 2, 16, 2 * LANE)
            return carry

        lax.fori_loop(0, per_half // 2, weight_part, 0)
        r1_cp[h] = send(wgp.at[h, :, 1 - core], r1.at[h], r1_id + h, core_s, r)

    rp_id, rm_id = recvs.take(2 * plus), recvs.take(2 * minus)
    rp_cp, rm_cp = {}, {}

    def local_sum(h, xl_, z_):
        at = xl_ * nz + z_
        return wgp[h, at, core].astype(F32) + r1[h, at].astype(F32)

    def ring_r(t, h):
        if t == 0:
            r1_cp[h].wait_recv()
        if t < minus:
            if t > 0:
                rm_cp[t - 1, h].wait_recv()
            for xl_ in range(2):
                value = local_sum(h, xl_, zat(t - minus))
                if t > 0:
                    value = value + rm[t - 1, h, xl_].astype(F32)
                sm[t, h, xl_] = value.astype(BF)
            rm_cp[t, h] = send(sm.at[t, h], rm.at[t, h], rm_id + 2 * t + h, zm_s, r)
        if t < plus:
            if t > 0:
                rp_cp[t - 1, h].wait_recv()
            for xl_ in range(2):
                value = local_sum(h, xl_, zat(plus - t))
                if t > 0:
                    value = value + rp[t - 1, h, xl_].astype(F32)
                sp[t, h, xl_] = value.astype(BF)
            rp_cp[t, h] = send(sp.at[t, h], rp.at[t, h], rp_id + 2 * t + h, zp_s, r)

    r4_id = recvs.take(4 * ny)
    r4_cp = []

    def finish(h):
        rm_cp[minus - 1, h].wait_recv()
        rp_cp[plus - 1, h].wait_recv()
        for sub in range(2):
            xl_ = 1 - xl if sub else xl
            done = local_sum(h, xl_, z) + rm[minus - 1, h, xl_].astype(F32) + rp[plus - 1, h, xl_].astype(F32)
            for p in range(h * quarter, (h + 1) * quarter):
                f4[2 * p + sub, 0] = done[:, lanes_of(main_block(p) - h * per_half)]
                f4[2 * p + sub, 1] = done[:, lanes_of(pair_block(p) - h * per_half)]
        for p in range(h * quarter, (h + 1) * quarter):
            for sub in range(2):
                if p or sub:
                    at = 2 * p + sub
                    r4_cp.append(
                        send(f4.at[at], r4.at[at], r4_id + at, xlp_s if sub else s, row(yat(off[p]), xh))
                    )

    gn_id = recvs.take(chans // 256)
    gn_cp = []

    def grad_part(i):
        value = jnp.zeros((gm.shape[1], 256), F32)
        for j in range(blocks // 2):
            g2 = jnp.concatenate([gm[2 * j], gm[2 * j + 1]], axis=1)
            here = wall[16 * i:16 * i + 16, :, lanes_of(2 * j, 2)].reshape(256, 256)
            value = value + lax.dot_general(
                g2, here, (((1,), (1,)), ((), ())), preferred_element_type=F32
            )
        gnp[:, 256 * i:256 * i + 256] = value
        gns[i] = value.astype(BF)
        gn_cp.append(send(gns.at[i], gnr.at[i], gn_id + i, s, row(y, 1 - xh)))

    def norm_back(i, carry):
        px = pl.ds(pl.multiple_of(i * width, width), width)
        other = jnp.concatenate([gnr[j, px, :] for j in range(chans // 256)], axis=1)
        scaled = (gnp[px, :] + other.astype(F32)) * gain[...]
        unit = mx[px, :]
        first = jnp.mean(scaled, axis=-1, keepdims=True)
        second = jnp.mean(scaled * unit, axis=-1, keepdims=True)
        gmx[3 + i] = (inv[px, 0:1] * (scaled - first - unit * second)).astype(BF)
        return carry

    def expand_back(i, carry):
        at = 4 * xh + i
        line = 8 * y - 3 + at
        ok = (line >= 0) & (line < height_all) & (col_ids >= 0)
        xp[i, 8:8 + width, :] = jnp.where(ok, gmx[at].astype(F32), 0.0)
        return carry

    out_cols = lax.broadcasted_iota(jnp.int32, (width, LANE), 0)

    def put_out(out, lanes, value):
        ok = (out_cols < wid) & (8 * y + 4 * xh + out < height)
        ig[out, :, lanes] = jnp.where(ok, value, 0.0).astype(BF)

    def conv_back(lane, carry):
        conv(4, True, lane, put_out)
        return carry

    weight_half(0)
    ring_w_step(4)
    ring_r(0, 0)
    weight_half(1)
    ring_w_step(5)
    ring_r(1, 0)
    ring_r(0, 1)
    ring_w_step(6)
    ring_r(2, 0)
    ring_r(1, 1)
    for cp in wc_cp:
        cp.wait_recv()
    for i in range(chans // 256):
        grad_part(i)
    ring_r(3, 0)
    ring_r(2, 1)
    ring_r(4, 0)
    ring_r(3, 1)
    ring_r(5, 0)
    ring_r(4, 1)
    for cp in gn_cp:
        cp.wait_recv()
    lax.fori_loop(0, 8, norm_back, 0)
    hb_id = recvs.take()
    hb_cp = send(
        gmx.at[pl.ds(8 - 5 * xh, 3)], gmx.at[pl.ds(11 * xh, 3)], hb_id, s, row(yat(1 - 2 * xh), xh)
    )
    finish(0)
    ring_r(5, 1)
    finish(1)
    hb_cp.wait_recv()
    lax.fori_loop(0, 10, expand_back, 0)
    lax.fori_loop(0, chunks, conv_back, 0)
    for cp in r4_cp:
        cp.wait_recv()
    r4[0] = f4[0]
    main = r4[0, 0]
    tails = [r4[0, 1], r4[2, 1]]
    for at in range(1, 2 * ny):
        main = main + r4[at, 0]
        if at not in (0, 2):
            tails[(at // 2) % 2] = tails[(at // 2) % 2] + r4[at, 1]
    tail = tails[0] + pltpu.roll(tails[1], LANE // 2, 1)
    wg[:, 0:LANE] = main / images
    wg[:, LANE:] = tail[:, 0:LANE // 2] / images

    for cp in started:
        cp.wait_send()
    assert slots.count <= ssem.shape[0] and recvs.count <= rsem.shape[0]


def local(ny, nz, images, activations, cotangent, proj_weight, kernel_taps, ln_gain, ln_shift, heights, widths):
    rows_dev, width, chans = activations.shape[1:]
    height_all, hidden = cotangent.shape[1], cotangent.shape[3]
    blocks = ny + ny // 2
    px = 2 * rows_dev * width
    plus, minus = (nz - 1) // 2, nz // 2
    cols = blocks * LANE
    vmem = pltpu.VMEM
    out = pl.pallas_call(
        functools.partial(kernel_body, ny, nz, float(images)),
        out_shape=(
            jax.ShapeDtypeStruct((rows_dev, width, chans), BF),
            jax.ShapeDtypeStruct((16, hidden), F32),
        ),
        in_specs=[pl.BlockSpec(memory_space=pltpu.SMEM)] * 2
        + [pl.BlockSpec(memory_space=pl.ANY)] * 2
        + [pl.BlockSpec(memory_space=vmem)] * 4,
        out_specs=[pl.BlockSpec(memory_space=vmem)] * 2,
        scratch_shapes=[
            vmem((14, width, chans), BF),
            vmem((14, width + 16, chans), F32),
            vmem((56, chans), F32),
            vmem((px, chans), F32),
            vmem((px, LANE), F32),
            vmem((px, chans), BF),
            vmem((height_all, width, hidden), BF),
            vmem((ny, px, LANE), BF),
            vmem((ny, px // 2, LANE), BF),
            vmem((blocks, px, LANE), BF),
            vmem((ny, px // 2, LANE), BF),
            vmem((16, 2 * LANE), BF),
            vmem((2 * ny, 16, 2 * LANE), BF),
            vmem((4 * nz, 16, cols), BF),
            vmem((2, 2 * nz, 2, 16, cols // 2), BF),
            vmem((2, 2 * nz, 16, cols // 2), BF),
            vmem((plus, 2, 2, 16, cols // 2), BF),
            vmem((minus, 2, 2, 16, cols // 2), BF),
            vmem((plus, 2, 2, 16, cols // 2), BF),
            vmem((minus, 2, 2, 16, cols // 2), BF),
            vmem((2 * ny, 2, 16, LANE), F32),
            vmem((2 * ny, 2, 16, LANE), F32),
            vmem((px, chans), F32),
            vmem((chans // 256, px, 256), BF),
            vmem((chans // 256, px, 256), BF),
            vmem((14, width, chans), BF),
            pltpu.SemaphoreType.DMA((192,)),
            pltpu.SemaphoreType.DMA((192,)),
            pltpu.SemaphoreType.DMA((3,)),
        ],
        compiler_params=pltpu.CompilerParams(
            collective_id=0, has_side_effects=True, vmem_limit_bytes=60 * 1024 * 1024
        ),
    )(
        heights, widths, activations[0], cotangent[0], proj_weight, kernel_taps,
        ln_gain.reshape(1, chans), ln_shift.reshape(1, chans),
    )
    return out[0][None], out[1]


def solution(mesh):
    ny = mesh.shape["rows"] // 2
    nz = mesh.shape["section"] // 4
    in_specs = (
        P("section", "rows", None, None),
        P("section", None, None, "rows"),
        P("section", "rows"),
        P(),
        P(),
        P(),
        P("section"),
        P("section"),
    )
    out_specs = (P("section", "rows", None, None), P("section", "rows"))
    body = functools.partial(local, ny, nz, mesh.shape["section"])
    return jax.shard_map(body, mesh=mesh, in_specs=in_specs, out_specs=out_specs, check_vma=False)
```

time: 114 us -> 89.6 us (0.79)
  the two profiles are of different devices: /device:TPU:6 before, /device:TPU:1 now
where the time goes in v2:
time: 89.6 us; the launch traced here: 89.3 us
  Pallas kernels  83.8 us (94%)
  local copies, waits for them, and re-layouts  3.48 us (4%)
  between operations  1.98 us (2%)
    pallas_call x1, Pallas kernels, local(): pl.pallas_call(functools.partial(kernel_body, ny, nz, float(images)), out...  83.8 us
    unnamed x8, local copies, waits for them, and re-layouts  2.32 us

profile of v2, /device:TPU:1, one launch (start us, length us, event | category | flops | bytes accessed | tf_op | source)
XLA Modules:
  0.0 89.3 jit_solution(1123851511080898492)
XLA Ops:
  0.6 0.0 copy-start.1
  1.9 0.0 copy-start.2
  2.0 0.0 copy-done.1
  2.0 0.6 reshape.10.gain
  2.5 0.1 copy-done.2
  2.6 0.6 reshape.11.shift
  3.2 83.8 %shard_map.95 = (bf16[4,32,768]{2,1,0:T(8,128)(2,1)}, f32[16,192]{1,0:T(8,128)}) custom-call(s32[1]{0:T(128)S(6)} %copy.12.h_ref, s32[1]{0:T(128)S(6)} %copy.13.w_ref, bf16[4,32,768]{2,1,0:T(8,128)(2,1)} %bitcast.4, bf16[64,32,192]{2,1,0:T(8,128)(2,1)} %bitcast.3, bf16[16,192]{1,0:T(8,128)(2,1)} %proj.1, bf16[49,768]{1,0:T(8,128)(2,1)} %taps.1, ...), custom_call_target="tpu_custom_call" | custom-call | tf_op jit(solution)/shard_map/pallas_call | solution.py:451
  87.1 0.0 copy-start
  87.1 1.6 %copy.14 = bf16[1,4,32,768]{3,2,1,0:T(8,128)(2,1)} copy(bf16[1,4,32,768]{3,2,1,0:T(8,128)(2,1)} %bitcast.5) | data formatting | bytes 393216
  88.7 0.0 copy-done
  88.7 0.6 copy.15
Async XLA Ops:
  0.6 1.3 %copy-start.1 = (f32[768]{0:T(1024)S(1)}, f32[768]{0:T(1024)}, u32[]{:S(2)}) copy-start(f32[768]{0:T(1024)} %param.12) | copy-start | bytes 9220
  1.9 0.7 copy-start.2
  87.1 1.6 %copy-start = (f32[16,192]{1,0:T(8,128)S(1)}, f32[16,192]{1,0:T(8,128)}, u32[]{:S(2)}) copy-start(f32[16,192]{1,0:T(8,128)} %get-tuple-element.9) | copy-start | bytes 36868

commit v3 on v2

--- a/solution.py
+++ b/solution.py
@@ -25,10 +25,10 @@
 
 def kernel_body(
     ny, nz, images,
-    h_ref, w_ref, act, cot, proj, taps, gain, shift,
+    h_ref, w_ref, act, cot, proj, taps, gain_in, shift_in,
     ig, wg,
     actx, xp, tf, mx, inv, nrm, cbuf, g_a, g_b, gm, gb, wq, ws1, wall, wgp, r1, sp, sm, rp, rm,
-    f4, r4, gnp, gns, gnr, gmx, ssem, rsem, lsem,
+    f4, r4, gnp, gns, gnr, gmx, gain, shift, qa_p, qa_m, qh_p, qh_m, qg_p, qg_m, ssem, rsem, lsem,
 ):
     s = lax.axis_index("section")
     r = lax.axis_index("rows")
@@ -46,6 +46,7 @@
     per_half = quarter + quarter // 2
     blocks = 2 * per_half
     off = sorted(range(ny), key=lambda k: min(k, ny - k))
+    own = off.index(0)
 
     def main_block(p):
         return per_half * (p // quarter) + p % quarter
@@ -83,12 +84,13 @@
 
     core_s = sec(xl, z, 1 - core)
     xlp_s = sec(1 - xl, z, core)
+    xh_p = lax.rem(xh + xl, 2)
     zp_s = sec(xl, zat(1), core)
     zm_s = sec(xl, zat(-1), core)
 
     barrier = pltpu.get_barrier_semaphore()
     peers = [(xs, row(yat(k), xh)) for k in range(ny) for xs in (s, xlp_s) if not (k == 0 and xs is s)]
-    peers += [(s, row(y, 1 - xh)), (s, row(yat(1), 1 - xh)), (s, row(yat(-1), 1 - xh))]
+    peers += [(xlp_s, row(yat(k), 1 - xh)) for k in (0, 1, -1)]
     peers += [(core_s, r), (zp_s, r), (zm_s, r)]
     for s_, r_ in peers:
         pl.semaphore_signal(
@@ -102,9 +104,48 @@
     own_act.start()
     wq[:, LANE:] = jnp.zeros((16, LANE), BF)
     wq[:, 0:proj.shape[1]] = proj[...]
-    ws1[0] = wq[...]
+    ws1[2 * own] = wq[...]
+    pl.semaphore_wait(barrier, len(peers))
+
+    w1 = recvs.take(2 * ny)
+    w1_cp = []
+    for p in range(ny):
+        for sub in range(2):
+            if p != own or sub:
+                w1_cp.append(
+                    send(wq, ws1.at[2 * p + sub], w1 + 2 * p + sub, xlp_s if sub else s, row(yat(-off[p]), xh))
+                )
+
+    halo_y = yat(2 * xh - 1)
+    nexts, befores = (xlp_s, row(y, xh_p)), (xlp_s, row(y, 1 - xh_p))
+    relay_id = recvs.take(4)
+    pair_p = send(act.at[pl.ds(0, 2)], qa_p, relay_id, *nexts)
+    pair_m = send(act.at[pl.ds(2, 2)], qa_m, relay_id + 1, *befores)
+    halo_p = send(act.at[pl.ds(xh, 2)], qh_p, relay_id + 2, *nexts)
+    halo_m = send(act.at[pl.ds(xh + 2, 1)], qh_m, relay_id + 3, *befores)
+    direct = send(act.at[pl.ds(xh, 3)], actx.at[pl.ds(11 * (1 - xh), 3)], recvs.take(), s, row(halo_y, xh))
+    act_cp = [direct]
+
+    def relay_pairs():
+        pair_p.wait_recv()
+        at = 3 + 4 * (1 - xh_p)
+        act_cp.append(send(qa_p, actx.at[pl.ds(at, 2)], recvs.take(), *nexts))
+        pair_m.wait_recv()
+        at = 5 + 4 * xh_p
+        act_cp.append(send(qa_m, actx.at[pl.ds(at, 2)], recvs.take(), *befores))
+
+    def relay_halos():
+        halo_p.wait_recv()
+        to = row(yat(1 - 2 * xh_p), xh_p)
+        act_cp.append(send(qh_p, actx.at[pl.ds(11 * xh_p, 2)], recvs.take(), xlp_s, to))
+        halo_m.wait_recv()
+        to = row(yat(2 * xh_p - 1), 1 - xh_p)
+        act_cp.append(send(qh_m, actx.at[pl.ds(11 * (1 - xh_p) + 2, 1)], recvs.take(), xlp_s, to))
+
     tf[pl.ds(0, 49), :] = taps[...].astype(F32)
     xp[...] = jnp.zeros_like(xp)
+    gain[...] = gain_in[...].reshape(1, chans)
+    shift[...] = shift_in[...].reshape(1, chans)
     height, wid = h_ref[0], w_ref[0]
     own_cot.wait()
     cols3 = lax.broadcasted_iota(jnp.int32, (8, width, LANE), 1)
@@ -123,37 +164,6 @@
         return carry
 
     lax.fori_loop(0, ny, pack, 0)
-    pl.semaphore_wait(barrier, len(peers))
-
-    w1 = recvs.take(2 * ny)
-    w1_cp = []
-    for p in range(ny):
-        for sub in range(2):
-            if p or sub:
-                w1_cp.append(
-                    send(wq, ws1.at[2 * p + sub], w1 + 2 * p + sub, xlp_s if sub else s, row(yat(-off[p]), xh))
-                )
-
-    a_pair, a_halo = recvs.take(), recvs.take(2)
-    pair_cp = send(act, actx.at[pl.ds(3 + 4 * xh, 4)], a_pair, s, row(y, 1 - xh))
-    halo_y = yat(2 * xh - 1)
-    for to in range(2):
-        halo_cp = send(
-            act.at[pl.ds(xh, 3)], actx.at[pl.ds(11 * (1 - xh), 3)], a_halo + xh, s, row(halo_y, to)
-        )
-
-    ga_id, gb_id = recvs.take(ny), recvs.take(ny)
-    g_cp = {}
-    for p in range(1, ny):
-        to = yat(-off[p])
-        g_cp[p] = (
-            send(g_a.at[to], gm.at[main_block(p)], ga_id + p, s, row(to, xh)),
-            send(g_b.at[to], gb.at[p], gb_id + p, s, row(to, xh)),
-        )
-    own_ga = pltpu.make_async_copy(g_a.at[y], gm.at[0], lsem.at[1])
-    own_gb = pltpu.make_async_copy(g_b.at[y], gb.at[0], lsem.at[2])
-    own_ga.start()
-    own_gb.start()
 
     wp_id, wm_id, wc_id = recvs.take(2 * plus), recvs.take(2 * minus), recvs.take(2 * nz)
     wc_cp = []
@@ -194,15 +204,18 @@
         for sub in range(2):
             to_core(sub, z)
 
+    def ring_w_part(t, sub):
+        if t <= plus:
+            wp_cp[t - 1, sub].wait_recv()
+        wm_cp[t - 1, sub].wait_recv()
+        ring_w(t, sub)
+        if t <= plus:
+            to_core(sub, zat(-t))
+        to_core(sub, zat(t))
+
     def ring_w_step(t):
-        for sub in range(2):
-            if t <= plus:
-                wp_cp[t - 1, sub].wait_recv()
-            wm_cp[t - 1, sub].wait_recv()
-            ring_w(t, sub)
-            if t <= plus:
-                to_core(sub, zat(-t))
-            to_core(sub, zat(t))
+        ring_w_part(t, 0)
+        ring_w_part(t, 1)
 
     col_ids = lax.broadcasted_iota(jnp.int32, (width, chans), 0)
 
@@ -222,15 +235,29 @@
         for out in range(rows_out):
             put(out, lanes, total[out])
 
+    relay_pairs()
     ring_w_open()
+    relay_halos()
+
     ring_w_step(1)
-    pair_cp.wait_recv()
-    for i in range(2):
-        pltpu.make_async_remote_copy(
-            src_ref=act.at[pl.ds(xh, 3)], dst_ref=actx.at[pl.ds(11 * (1 - i), 3)],
-            send_sem=ssem.at[0], recv_sem=rsem.at[a_halo + i],
-            device_id={"section": s, "rows": row(halo_y, 0)}, device_id_type=pl.DeviceIdType.MESH,
-        ).wait_recv()
+
+    ga_id, gb_id = recvs.take(ny), recvs.take(ny)
+    g_cp = {}
+    for p in range(ny):
+        if p == own:
+            continue
+        to = yat(-off[p])
+        g_cp[p] = (
+            send(g_a.at[to], gm.at[main_block(p)], ga_id + p, s, row(to, xh)),
+            send(g_b.at[to], gb.at[p], gb_id + p, s, row(to, xh)),
+        )
+    own_ga = pltpu.make_async_copy(g_a.at[y], gm.at[main_block(own)], lsem.at[1])
+    own_gb = pltpu.make_async_copy(g_b.at[y], gb.at[own], lsem.at[2])
+    own_ga.start()
+    own_gb.start()
+
+    for cp in act_cp:
+        cp.wait_recv()
     own_act.wait()
 
     def expand(i, carry):
@@ -251,7 +278,6 @@
     lax.fori_loop(0, chunks // 2, conv_fwd, 0)
     ring_w_step(2)
     lax.fori_loop(chunks // 2, chunks, conv_fwd, 0)
-    ring_w_step(3)
 
     def norm(i, carry):
         px = pl.ds(pl.multiple_of(i * width, width), width)
@@ -266,18 +292,20 @@
         return carry
 
     lax.fori_loop(0, 8, norm, 0)
-
-    r1_id = recvs.take(2)
+    ring_w_step(3)
+
+    r1_id = recvs.take(2 * nz)
     r1_cp = {}
+    order_z = [d for t in range(minus) for d in ((t - minus, plus - t) if t < plus else (t - minus,))] + [0]
 
     def weight_half(h):
         for p in range(h * quarter, (h + 1) * quarter):
-            if p:
+            if p != own:
                 g_cp[p][0].wait_recv()
                 g_cp[p][1].wait_recv()
-        if h == 0:
-            own_ga.wait()
-            own_gb.wait()
+            else:
+                own_ga.wait()
+                own_gb.wait()
         for p in range(h * quarter, (h + 1) * quarter, 2):
             first, second = gb[p].astype(F32), gb[p + 1].astype(F32)
             at = pair_block(p)
@@ -292,23 +320,26 @@
                 part = lax.dot_general(
                     nrm[:, i * 256:(i + 1) * 256], g2, (((0,), (0,)), ((), ())), preferred_element_type=F32
                 )
-                wgp[h, 8 * i:8 * i + 8, :, :, lanes] = part.astype(BF).reshape(8, 2, 16, 2 * LANE)
+                for q in range(2):
+                    xl_, z_ = divmod(8 * i + 4 * q, nz)
+                    piece = part[128 * q:128 * q + 128].astype(BF).reshape(4, 2, 16, 2 * LANE)
+                    wgp[h, xl_, z_:z_ + 4, :, :, lanes] = piece
             return carry
 
         lax.fori_loop(0, per_half // 2, weight_part, 0)
-        r1_cp[h] = send(wgp.at[h, :, 1 - core], r1.at[h], r1_id + h, core_s, r)
+        for d in order_z:
+            at = zat(d)
+            r1_cp[h, d] = send(wgp.at[h, :, at, 1 - core], r1.at[h, :, at], r1_id + h * nz + d + minus, core_s, r)
 
     rp_id, rm_id = recvs.take(2 * plus), recvs.take(2 * minus)
     rp_cp, rm_cp = {}, {}
 
     def local_sum(h, xl_, z_):
-        at = xl_ * nz + z_
-        return wgp[h, at, core].astype(F32) + r1[h, at].astype(F32)
+        return wgp[h, xl_, z_, core].astype(F32) + r1[h, xl_, z_].astype(F32)
 
     def ring_r(t, h):
-        if t == 0:
-            r1_cp[h].wait_recv()
         if t < minus:
+            r1_cp[h, t - minus].wait_recv()
             if t > 0:
                 rm_cp[t - 1, h].wait_recv()
             for xl_ in range(2):
@@ -318,6 +349,7 @@
                 sm[t, h, xl_] = value.astype(BF)
             rm_cp[t, h] = send(sm.at[t, h], rm.at[t, h], rm_id + 2 * t + h, zm_s, r)
         if t < plus:
+            r1_cp[h, plus - t].wait_recv()
             if t > 0:
                 rp_cp[t - 1, h].wait_recv()
             for xl_ in range(2):
@@ -331,6 +363,7 @@
     r4_cp = []
 
     def finish(h):
+        r1_cp[h, 0].wait_recv()
         rm_cp[minus - 1, h].wait_recv()
         rp_cp[plus - 1, h].wait_recv()
         for sub in range(2):
@@ -341,14 +374,15 @@
                 f4[2 * p + sub, 1] = done[:, lanes_of(pair_block(p) - h * per_half)]
         for p in range(h * quarter, (h + 1) * quarter):
             for sub in range(2):
-                if p or sub:
+                if p != own or sub:
                     at = 2 * p + sub
                     r4_cp.append(
                         send(f4.at[at], r4.at[at], r4_id + at, xlp_s if sub else s, row(yat(off[p]), xh))
                     )
 
-    gn_id = recvs.take(chans // 256)
-    gn_cp = []
+    gn_id = recvs.take(4 * (chans // 256))
+    gn_first, gn_cp = [], []
+    mid = gm.shape[1] // 2
 
     def grad_part(i):
         value = jnp.zeros((gm.shape[1], 256), F32)
@@ -360,7 +394,14 @@
             )
         gnp[:, 256 * i:256 * i + 256] = value
         gns[i] = value.astype(BF)
-        gn_cp.append(send(gns.at[i], gnr.at[i], gn_id + i, s, row(y, 1 - xh)))
+        gn_first.append(send(gns.at[i, pl.ds(0, mid)], qg_p.at[i], gn_id + 4 * i, *nexts))
+        gn_first.append(send(gns.at[i, pl.ds(mid, mid)], qg_m.at[i], gn_id + 4 * i + 1, *befores))
+
+    def relay_grad(i):
+        gn_first[2 * i].wait_recv()
+        gn_cp.append(send(qg_p.at[i], gnr.at[i, pl.ds(0, mid)], gn_id + 4 * i + 2, *nexts))
+        gn_first[2 * i + 1].wait_recv()
+        gn_cp.append(send(qg_m.at[i], gnr.at[i, pl.ds(mid, mid)], gn_id + 4 * i + 3, *befores))
 
     def norm_back(i, carry):
         px = pl.ds(pl.multiple_of(i * width, width), width)
@@ -390,14 +431,14 @@
         return carry
 
     weight_half(0)
+    ring_r(0, 0)
     ring_w_step(4)
-    ring_r(0, 0)
+    ring_r(1, 0)
     weight_half(1)
     ring_w_step(5)
-    ring_r(1, 0)
     ring_r(0, 1)
+    ring_r(2, 0)
     ring_w_step(6)
-    ring_r(2, 0)
     ring_r(1, 1)
     for cp in wc_cp:
         cp.wait_recv()
@@ -405,6 +446,8 @@
         grad_part(i)
     ring_r(3, 0)
     ring_r(2, 1)
+    for i in range(chans // 256):
+        relay_grad(i)
     ring_r(4, 0)
     ring_r(3, 1)
     ring_r(5, 0)
@@ -424,13 +467,12 @@
     lax.fori_loop(0, chunks, conv_back, 0)
     for cp in r4_cp:
         cp.wait_recv()
-    r4[0] = f4[0]
-    main = r4[0, 0]
-    tails = [r4[0, 1], r4[2, 1]]
-    for at in range(1, 2 * ny):
-        main = main + r4[at, 0]
-        if at not in (0, 2):
-            tails[(at // 2) % 2] = tails[(at // 2) % 2] + r4[at, 1]
+    r4[2 * own] = f4[2 * own]
+    main, tails = None, [None, None]
+    for at in range(2 * ny):
+        main = r4[at, 0] if main is None else main + r4[at, 0]
+        odd = (at // 2) % 2
+        tails[odd] = r4[at, 1] if tails[odd] is None else tails[odd] + r4[at, 1]
     tail = tails[0] + pltpu.roll(tails[1], LANE // 2, 1)
     wg[:, 0:LANE] = main / images
     wg[:, LANE:] = tail[:, 0:LANE // 2] / images
@@ -451,8 +493,8 @@
     out = pl.pallas_call(
         functools.partial(kernel_body, ny, nz, float(images)),
         out_shape=(
-            jax.ShapeDtypeStruct((rows_dev, width, chans), BF),
-            jax.ShapeDtypeStruct((16, hidden), F32),
+            pltpu.VMEM((rows_dev, width, chans), BF),
+            pltpu.VMEM((16, hidden), F32),
         ),
         in_specs=[pl.BlockSpec(memory_space=pltpu.SMEM)] * 2
         + [pl.BlockSpec(memory_space=pl.ANY)] * 2
@@ -473,8 +515,8 @@
             vmem((16, 2 * LANE), BF),
             vmem((2 * ny, 16, 2 * LANE), BF),
             vmem((4 * nz, 16, cols), BF),
-            vmem((2, 2 * nz, 2, 16, cols // 2), BF),
-            vmem((2, 2 * nz, 16, cols // 2), BF),
+            vmem((2, 2, nz, 2, 16, cols // 2), BF),
+            vmem((2, 2, nz, 16, cols // 2), BF),
             vmem((plus, 2, 2, 16, cols // 2), BF),
             vmem((minus, 2, 2, 16, cols // 2), BF),
             vmem((plus, 2, 2, 16, cols // 2), BF),
@@ -485,8 +527,16 @@
             vmem((chans // 256, px, 256), BF),
             vmem((chans // 256, px, 256), BF),
             vmem((14, width, chans), BF),
-            pltpu.SemaphoreType.DMA((192,)),
-            pltpu.SemaphoreType.DMA((192,)),
+            vmem((1, chans), F32),
+            vmem((1, chans), F32),
+            vmem((2, width, chans), BF),
+            vmem((2, width, chans), BF),
+            vmem((2, width, chans), BF),
+            vmem((1, width, chans), BF),
+            vmem((chans // 256, px // 2, 256), BF),
+            vmem((chans // 256, px // 2, 256), BF),
+            pltpu.SemaphoreType.DMA((224,)),
+            pltpu.SemaphoreType.DMA((224,)),
             pltpu.SemaphoreType.DMA((3,)),
         ],
         compiler_params=pltpu.CompilerParams(
@@ -494,7 +544,7 @@
         ),
     )(
         heights, widths, activations[0], cotangent[0], proj_weight, kernel_taps,
-        ln_gain.reshape(1, chans), ln_shift.reshape(1, chans),
+        ln_gain, ln_shift,
     )
     return out[0][None], out[1]
 

time: 89.6 us -> 89.2 us (level)
  the two profiles are of different devices: /device:TPU:1 before, /device:TPU:6 now
where the time goes in v3:
time: 89.2 us; the launch traced here: 89 us
  Pallas kernels  85.8 us (96%)
  between operations  1.93 us (2%)
  local copies, waits for them, and re-layouts  1.28 us (1%)
    pallas_call x1, Pallas kernels, local(): pl.pallas_call(functools.partial(kernel_body, ny, nz, float(images)), out...  85.8 us

profile of v3, /device:TPU:6, one launch (start us, length us, event | category | flops | bytes accessed | tf_op | source)
XLA Modules:
  0.0 89.0 jit_solution(2725831532814632943)
XLA Ops:
  1.9 85.8 %shard_map.95 = (bf16[4,32,768]{2,1,0:T(8,128)(2,1)S(1)}, f32[16,192]{1,0:T(8,128)S(1)}) custom-call(s32[1]{0:T(128)S(6)} %copy.14.h_ref, s32[1]{0:T(128)S(6)} %copy.15.w_ref, bf16[4,32,768]{2,1,0:T(8,128)(2,1)} %bitcast.5, bf16[64,32,192]{2,1,0:T(8,128)(2,1)} %bitcast.4, bf16[16,192]{1,0:T(8,128)(2,1)} %proj.1, bf16[49,768]{1,0:T(8,128)(2,1)} %taps.1, ...), custom_call_target="tpu_custom_call" | custom-call | tf_op jit(solution)/shard_map/pallas_call | solution.py:493
  87.7 0.7 copy.12
  88.4 0.6 copy.13

commit v4 on v3

--- a/solution.py
+++ b/solution.py
@@ -239,22 +239,26 @@
     ring_w_open()
     relay_halos()
 
-    ring_w_step(1)
-
     ga_id, gb_id = recvs.take(ny), recvs.take(ny)
     g_cp = {}
-    for p in range(ny):
-        if p == own:
-            continue
-        to = yat(-off[p])
-        g_cp[p] = (
-            send(g_a.at[to], gm.at[main_block(p)], ga_id + p, s, row(to, xh)),
-            send(g_b.at[to], gb.at[p], gb_id + p, s, row(to, xh)),
-        )
+
+    def send_half(h):
+        for p in range(h * quarter, (h + 1) * quarter):
+            if p == own:
+                continue
+            to = yat(-off[p])
+            g_cp[p] = (
+                send(g_a.at[to], gm.at[main_block(p)], ga_id + p, s, row(to, xh)),
+                send(g_b.at[to], gb.at[p], gb_id + p, s, row(to, xh)),
+            )
+
+    send_half(0)
     own_ga = pltpu.make_async_copy(g_a.at[y], gm.at[main_block(own)], lsem.at[1])
     own_gb = pltpu.make_async_copy(g_b.at[y], gb.at[own], lsem.at[2])
     own_ga.start()
     own_gb.start()
+    ring_w_step(1)
+    send_half(1)
 
     for cp in act_cp:
         cp.wait_recv()
@@ -431,19 +435,19 @@
         return carry
 
     weight_half(0)
+    ring_w_step(4)
     ring_r(0, 0)
-    ring_w_step(4)
     ring_r(1, 0)
+    ring_w_step(5)
     weight_half(1)
-    ring_w_step(5)
     ring_r(0, 1)
     ring_r(2, 0)
     ring_w_step(6)
-    ring_r(1, 1)
     for cp in wc_cp:
         cp.wait_recv()
     for i in range(chans // 256):
         grad_part(i)
+    ring_r(1, 1)
     ring_r(3, 0)
     ring_r(2, 1)
     for i in range(chans // 256):

time: 89.2 us -> 90.2 us (1.011)
  no operation moved by 1% of the time
where the time goes in v4:
time: 90.2 us; the launch traced here: 89.1 us
  Pallas kernels  85.9 us (95%)
  between operations  1.93 us (2%)
  local copies, waits for them, and re-layouts  1.28 us (1%)
    pallas_call x1, Pallas kernels, local(): pl.pallas_call(functools.partial(kernel_body, ny, nz, float(images)), out...  85.9 us

profile of v4, /device:TPU:6, one launch (start us, length us, event | category | flops | bytes accessed | tf_op | source)
XLA Modules:
  0.0 89.1 jit_solution(18349876449224789471)
XLA Ops:
  1.9 85.9 %shard_map.95 = (bf16[4,32,768]{2,1,0:T(8,128)(2,1)S(1)}, f32[16,192]{1,0:T(8,128)S(1)}) custom-call(s32[1]{0:T(128)S(6)} %copy.14.h_ref, s32[1]{0:T(128)S(6)} %copy.15.w_ref, bf16[4,32,768]{2,1,0:T(8,128)(2,1)} %bitcast.5, bf16[64,32,192]{2,1,0:T(8,128)(2,1)} %bitcast.4, bf16[16,192]{1,0:T(8,128)(2,1)} %proj.1, bf16[49,768]{1,0:T(8,128)(2,1)} %taps.1, ...), custom_call_target="tpu_custom_call" | custom-call | tf_op jit(solution)/shard_map/pallas_call | solution.py:497
  87.8 0.7 copy.12
  88.5 0.6 copy.13

commit v5 on v2

--- a/solution.py
+++ b/solution.py
@@ -25,10 +25,10 @@
 
 def kernel_body(
     ny, nz, images,
-    h_ref, w_ref, act, cot, proj, taps, gain, shift,
+    h_ref, w_ref, act, cot, proj, taps, gain_in, shift_in,
     ig, wg,
     actx, xp, tf, mx, inv, nrm, cbuf, g_a, g_b, gm, gb, wq, ws1, wall, wgp, r1, sp, sm, rp, rm,
-    f4, r4, gnp, gns, gnr, gmx, ssem, rsem, lsem,
+    f4, r4, gnp, gns, gnr, gmx, gain, shift, ssem, rsem, lsem,
 ):
     s = lax.axis_index("section")
     r = lax.axis_index("rows")
@@ -105,6 +105,8 @@
     ws1[0] = wq[...]
     tf[pl.ds(0, 49), :] = taps[...].astype(F32)
     xp[...] = jnp.zeros_like(xp)
+    gain[...] = gain_in[...].reshape(1, chans)
+    shift[...] = shift_in[...].reshape(1, chans)
     height, wid = h_ref[0], w_ref[0]
     own_cot.wait()
     cols3 = lax.broadcasted_iota(jnp.int32, (8, width, LANE), 1)
@@ -141,19 +143,6 @@
         halo_cp = send(
             act.at[pl.ds(xh, 3)], actx.at[pl.ds(11 * (1 - xh), 3)], a_halo + xh, s, row(halo_y, to)
         )
-
-    ga_id, gb_id = recvs.take(ny), recvs.take(ny)
-    g_cp = {}
-    for p in range(1, ny):
-        to = yat(-off[p])
-        g_cp[p] = (
-            send(g_a.at[to], gm.at[main_block(p)], ga_id + p, s, row(to, xh)),
-            send(g_b.at[to], gb.at[p], gb_id + p, s, row(to, xh)),
-        )
-    own_ga = pltpu.make_async_copy(g_a.at[y], gm.at[0], lsem.at[1])
-    own_gb = pltpu.make_async_copy(g_b.at[y], gb.at[0], lsem.at[2])
-    own_ga.start()
-    own_gb.start()
 
     wp_id, wm_id, wc_id = recvs.take(2 * plus), recvs.take(2 * minus), recvs.take(2 * nz)
     wc_cp = []
@@ -223,6 +212,20 @@
             put(out, lanes, total[out])
 
     ring_w_open()
+
+    ga_id, gb_id = recvs.take(ny), recvs.take(ny)
+    g_cp = {}
+    for p in range(1, ny):
+        to = yat(-off[p])
+        g_cp[p] = (
+            send(g_a.at[to], gm.at[main_block(p)], ga_id + p, s, row(to, xh)),
+            send(g_b.at[to], gb.at[p], gb_id + p, s, row(to, xh)),
+        )
+    own_ga = pltpu.make_async_copy(g_a.at[y], gm.at[0], lsem.at[1])
+    own_gb = pltpu.make_async_copy(g_b.at[y], gb.at[0], lsem.at[2])
+    own_ga.start()
+    own_gb.start()
+
     ring_w_step(1)
     pair_cp.wait_recv()
     for i in range(2):
@@ -248,10 +251,13 @@
         conv(8, False, lane, put_mixed)
         return carry
 
-    lax.fori_loop(0, chunks // 2, conv_fwd, 0)
     ring_w_step(2)
-    lax.fori_loop(chunks // 2, chunks, conv_fwd, 0)
+    lax.fori_loop(0, chunks // 3, conv_fwd, 0)
     ring_w_step(3)
+    lax.fori_loop(chunks // 3, 2 * chunks // 3, conv_fwd, 0)
+    ring_w_step(4)
+    lax.fori_loop(2 * chunks // 3, chunks, conv_fwd, 0)
+    ring_w_step(5)
 
     def norm(i, carry):
         px = pl.ds(pl.multiple_of(i * width, width), width)
@@ -390,25 +396,20 @@
         return carry
 
     weight_half(0)
-    ring_w_step(4)
+    ring_w_step(6)
     ring_r(0, 0)
     weight_half(1)
-    ring_w_step(5)
-    ring_r(1, 0)
-    ring_r(0, 1)
-    ring_w_step(6)
-    ring_r(2, 0)
-    ring_r(1, 1)
     for cp in wc_cp:
         cp.wait_recv()
     for i in range(chans // 256):
         grad_part(i)
+    ring_r(0, 1)
+    ring_r(1, 0)
+    ring_r(1, 1)
+    ring_r(2, 0)
+    ring_r(2, 1)
     ring_r(3, 0)
-    ring_r(2, 1)
-    ring_r(4, 0)
     ring_r(3, 1)
-    ring_r(5, 0)
-    ring_r(4, 1)
     for cp in gn_cp:
         cp.wait_recv()
     lax.fori_loop(0, 8, norm_back, 0)
@@ -416,8 +417,11 @@
     hb_cp = send(
         gmx.at[pl.ds(8 - 5 * xh, 3)], gmx.at[pl.ds(11 * xh, 3)], hb_id, s, row(yat(1 - 2 * xh), xh)
     )
+    ring_r(4, 0)
+    ring_r(4, 1)
+    ring_r(5, 0)
+    ring_r(5, 1)
     finish(0)
-    ring_r(5, 1)
     finish(1)
     hb_cp.wait_recv()
     lax.fori_loop(0, 10, expand_back, 0)
@@ -451,8 +455,8 @@
     out = pl.pallas_call(
         functools.partial(kernel_body, ny, nz, float(images)),
         out_shape=(
-            jax.ShapeDtypeStruct((rows_dev, width, chans), BF),
-            jax.ShapeDtypeStruct((16, hidden), F32),
+            pltpu.VMEM((rows_dev, width, chans), BF),
+            pltpu.VMEM((16, hidden), F32),
         ),
         in_specs=[pl.BlockSpec(memory_space=pltpu.SMEM)] * 2
         + [pl.BlockSpec(memory_space=pl.ANY)] * 2
@@ -485,6 +489,8 @@
             vmem((chans // 256, px, 256), BF),
             vmem((chans // 256, px, 256), BF),
             vmem((14, width, chans), BF),
+            vmem((1, chans), F32),
+            vmem((1, chans), F32),
             pltpu.SemaphoreType.DMA((192,)),
             pltpu.SemaphoreType.DMA((192,)),
             pltpu.SemaphoreType.DMA((3,)),
@@ -494,7 +500,7 @@
         ),
     )(
         heights, widths, activations[0], cotangent[0], proj_weight, kernel_taps,
-        ln_gain.reshape(1, chans), ln_shift.reshape(1, chans),
+        ln_gain, ln_shift,
     )
     return out[0][None], out[1]
 

time: 89.6 us -> 85.4 us (0.953)
  the two profiles are of different devices: /device:TPU:1 before, /device:TPU:6 now
where the time goes in v5:
time: 85.4 us; the launch traced here: 84.7 us
  Pallas kernels  81.5 us (95%)
  between operations  1.93 us (2%)
  local copies, waits for them, and re-layouts  1.28 us (1%)
    pallas_call x1, Pallas kernels, local(): pl.pallas_call(functools.partial(kernel_body, ny, nz, float(images)), out...  81.5 us

profile of v5, /device:TPU:6, one launch (start us, length us, event | category | flops | bytes accessed | tf_op | source)
XLA Modules:
  0.0 84.7 jit_solution(16746118774378999502)
XLA Ops:
  1.9 81.5 %shard_map.95 = (bf16[4,32,768]{2,1,0:T(8,128)(2,1)S(1)}, f32[16,192]{1,0:T(8,128)S(1)}) custom-call(s32[1]{0:T(128)S(6)} %copy.14.h_ref, s32[1]{0:T(128)S(6)} %copy.15.w_ref, bf16[4,32,768]{2,1,0:T(8,128)(2,1)} %bitcast.5, bf16[64,32,192]{2,1,0:T(8,128)(2,1)} %bitcast.4, bf16[16,192]{1,0:T(8,128)(2,1)} %proj.1, bf16[49,768]{1,0:T(8,128)(2,1)} %taps.1, ...), custom_call_target="tpu_custom_call" | custom-call | tf_op jit(solution)/shard_map/pallas_call | solution.py:455
  83.5 0.7 copy.12
  84.1 0.6 copy.13
